TPU v7x, 256 devices: a whole 4x4x8 slice. The times are simulated.
256 devices in a mesh: grp: 8 (over z_hi, y), row: 32 (over z_lo, x, core).
Axes of the slice: x: 4, y: 4, z: 8 (z_hi: 2, z_lo: 4; z = z_hi * 4 + z_lo), core: 2. Of those that a mesh axis runs over, the one named last changes fastest.
Arguments:
- points: bfloat16 [524288, 128], P(('grp', 'row')), as said below
- centers: bfloat16 [8192, 128], replicated, as said below
- inner_factor: bfloat16 [8192, 8192], P('row'), as said below
- outer_factor: bfloat16 [8192, 8192], P('row'), as said below
- iterate: float32 [64, 8192], P(None, 'row'), may hold values from -6 to 6
- residual: float32 [64, 8192], P(None, 'row'), as said below
- direction: float32 [64, 8192], P(None, 'row'), as said below
Outputs:
- next_iterate: float32 [64, 8192], P(None, 'row')
- next_residual: float32 [64, 8192], P(None, 'row')
- next_direction: float32 [64, 8192], P(None, 'row')
Inputs may be any that keep to these rules, and one draw needn't show every extreme that they name: `inner_factor`: upper triangular: zero below the diagonal, positive on it. `outer_factor`: upper triangular: zero below the diagonal, positive on it. `residual`: finite real values. `direction`: finite real values. `points`: finite real values. `centers`: finite real values.
All inputs are finite; a program needn't handle non-finite values.
Results may differ from a plain program's by a relative error of at most 0.0056.
Values may be sent and summed in bfloat16 or wider, within the bound.
No kernel may reach another device: no remote copies, remote signals or barrier semaphores. Data moves between devices by JAX's collectives and lax.ppermute only.
A program may use at most 64 MiB of HBM per device.

v0:
```python
import jax
import jax.numpy as jnp
from jax import lax
from jax.sharding import PartitionSpec as P

ridge_weight = 0.5


def kernel_rows(block_points, centers, center_norms):
    point_wide = block_points.astype(jnp.float32)
    point_norms = jnp.sum(point_wide * point_wide, axis=1)
    cross_term = lax.dot_general(
        block_points, centers, (((1,), (1,)), ((), ())), preferred_element_type=jnp.float32
    )
    distance = point_norms[:, None] + center_norms[None, :] - 2.0 * cross_term
    return jnp.exp(distance * (-4.0 / block_points.shape[1])).astype(jnp.bfloat16)


def local(points, centers, inner_factor, outer_factor, iterate, residual, direction):
    contract_last = (((1,), (1,)), ((), ()))
    own_rows = inner_factor.shape[0]
    targets = direction.shape[0]
    direction_half = direction.astype(jnp.bfloat16)
    columns = inner_factor
    inner_term = lax.dot_general(
        lax.all_gather(direction_half, "row", axis=1, tiled=True),
        columns,
        contract_last,
        preferred_element_type=jnp.float32,
    )
    inner_half = inner_term.astype(jnp.bfloat16)
    columns = outer_factor
    outer_rows = lax.dot_general(
        lax.all_gather(inner_half, "row", axis=1, tiled=True),
        columns,
        contract_last,
        preferred_element_type=jnp.float32,
    )
    outer_half = lax.all_gather(outer_rows.astype(jnp.bfloat16), "row", axis=1, tiled=True)
    center_wide = centers.astype(jnp.float32)
    center_norms = jnp.sum(center_wide * center_wide, axis=1)
    local_points = points.shape[0]
    block_rows = min(512, local_points)
    point_blocks = points.reshape(local_points // block_rows, block_rows, points.shape[1])

    def one_block(carried, block_points):
        kernel_block = kernel_rows(block_points, centers, center_norms)
        fitted = lax.dot_general(
            outer_half, kernel_block, contract_last, preferred_element_type=jnp.float32
        ).astype(jnp.bfloat16)
        return (carried + jnp.dot(fitted, kernel_block, preferred_element_type=jnp.float32), None)

    partial_sums, _ = lax.scan(
        one_block, jnp.zeros((targets, centers.shape[0]), jnp.float32), point_blocks
    )
    summed_all = lax.psum(partial_sums, ("grp", "row"))
    own_normal = lax.dynamic_slice_in_dim(summed_all, lax.axis_index("row") * own_rows, own_rows, 1)
    normal_half = own_normal.astype(jnp.bfloat16)
    point_count = local_points * lax.axis_size("grp") * lax.axis_size("row")
    outer_terms = jnp.dot(normal_half, outer_factor, preferred_element_type=jnp.float32)
    shaped = (
        lax.psum_scatter(outer_terms, "row", scatter_dimension=1, tiled=True) / point_count
        + ridge_weight * inner_term
    )
    shaped_half = shaped.astype(jnp.bfloat16)
    inner_terms = jnp.dot(shaped_half, inner_factor, preferred_element_type=jnp.float32)
    operator_image = lax.psum_scatter(inner_terms, "row", scatter_dimension=1, tiled=True)
    old_norm = lax.psum(jnp.sum(residual * residual, axis=1), "row")
    curvature = lax.psum(jnp.sum(direction * operator_image, axis=1), "row")
    step_size = old_norm / curvature
    next_residual = residual - step_size[:, None] * operator_image
    new_norm = lax.psum(jnp.sum(next_residual * next_residual, axis=1), "row")
    next_iterate = iterate + step_size[:, None] * direction
    next_direction = next_residual + (new_norm / old_norm)[:, None] * direction
    return (next_iterate, next_residual, next_direction)


def solution(mesh):
    placed = (
        P(("grp", "row"), None),
        P(),
        P("row", None),
        P("row", None),
        P(None, "row"),
        P(None, "row"),
        P(None, "row"),
    )
    return jax.shard_map(
        local,
        mesh=mesh,
        in_specs=placed,
        out_specs=(P(None, "row"), P(None, "row"), P(None, "row")),
        check_vma=False,
    )
```

profile of v0, /device:TPU:1, one launch (start us, length us, event | category | flops | bytes accessed | tf_op | source)
XLA Modules:
  0.0 819.4 jit_solution(775019206389307324)
XLA Ops:
  7.2 0.0 all-gather.4.cloned.1.call-start
  7.2 1.5 convert_element_type.29
  8.7 0.0 all-gather.4.cloned.1.call-update
  8.7 0.0 all-gather.6.cloned.1.call-start
  8.7 66.0 %all-gather.4.cloned.1.call-done = bf16[64,8192]{1,0:T(8,128)(2,1)} async-done(((bf16[64,256]{1,0:T(8,128)(2,1)}), bf16[64,8192]{1,0:T(8,128)(2,1)}) %all-gather.4.cloned.1.call-update) | async-done | bytes 1048592 | tf_op jit(solution)/shard_map/all_gather | solution.py:26
  74.8 4.5 fusion.10
  79.3 0.0 all-gather.6.cloned.1.call-update
  79.3 0.0 all-gather.8.cloned.1.call-start
  79.4 59.4 %all-gather.6.cloned.1.call-done = bf16[64,8192]{1,0:T(8,128)(2,1)} async-done(((bf16[64,256]{1,0:T(8,128)(2,1)}), bf16[64,8192]{1,0:T(8,128)(2,1)}) %all-gather.6.cloned.1.call-update) | async-done | bytes 1048592 | tf_op jit(solution)/shard_map/all_gather | solution.py:34
  138.7 4.5 convolution_convert_fusion.1
  143.2 0.0 all-gather.8.cloned.1.call-update
  143.3 0.2 reduce-scatter.3.cloned.1.call-start
  143.5 2.7 multiply_reduce_fusion.1
  146.3 56.4 %all-gather.8.cloned.1.call-done = bf16[64,8192]{1,0:T(8,128)(2,1)} async-done(((bf16[64,256]{1,0:T(8,128)(2,1)}), bf16[64,8192]{1,0:T(8,128)(2,1)}) %all-gather.8.cloned.1.call-update) | async-done | bytes 1048592 | tf_op jit(solution)/shard_map/all_gather | solution.py:39
  202.7 87.9 %while.11 = (s32[]{:T(128)}, f32[64,8192]{1,0:T(8,128)S(1)}, bf16[4,512,128]{2,1,0:T(8,128)(2,1)}, f32[8192]{0:T(1024)S(1)}, bf16[8192,128]{1,0:T(8,128)(2,1)}, ...) while((s32[]{:T(128)}, f32[64,8192]{1,0:T(8,128)S(1)}, bf16[4,512,128]{2,1,0:T(8,128)(2,1)}, ...), condition=%wide.region_5.6_spmd.clone, body=%wide.region_3.0_spmd.clone.sunk | while | flops 2169732608 | bytes 28610700 | solution.py:53
  202.7 1.0 multiply_reduce_fusion.6
  203.7 0.0 copy-start
  203.7 9.0 %exponential_convert_fusion.2 = bf16[512,8192]{1,0:T(8,128)(2,1)} fusion(bf16[8192,128]{1,0:T(8,128)(2,1)} %get-tuple-element.134, f32[8192]{0:T(1024)S(1)} %get-tuple-element.133, f32[512]{0:T(512)S(1)} %multiply_reduce_fusion.6, bf16[4,512,128]{2,1,0:T(8,128)(2,1)} %get-tuple-element.132, s32[]{:T(128)S(6)} %copy.12), kind=kOutput, calls=%fused_computation.clone.1 | convolution fusion | flops 1094713344 | bytes 10651652 | tf_op jit(solution)/shard_map/while/body/eval_jaxpr/dot_general | solution.py:12
  212.8 0.0 copy-done
  212.8 11.9 %convolution_add_fusion.2 = f32[64,8192]{1,0:T(8,128)S(1)} fusion(bf16[512,8192]{1,0:T(8,128)(2,1)} %exponential_convert_fusion.2, f32[64,8192]{1,0:T(8,128)S(1)} %get-tuple-element.123, pred[]{:T(512)S(6)} %compare.3, bf16[64,8192]{1,0:T(8,128)(2,1)S(1)} %copy-done), kind=kOutput, calls=%fused_computation.1.clone.1 | convolution fusion | flops 1074823168 | bytes 13631489 | tf_op jit(solution)/shard_map/while/body/eval_jaxpr/dot_general | solution.py:51
  224.7 1.1 multiply_reduce_fusion.6
  225.7 0.0 copy-start
  225.7 9.0 %exponential_convert_fusion.2 = bf16[512,8192]{1,0:T(8,128)(2,1)} fusion(bf16[8192,128]{1,0:T(8,128)(2,1)} %get-tuple-element.134, f32[8192]{0:T(1024)S(1)} %get-tuple-element.133, f32[512]{0:T(512)S(1)} %multiply_reduce_fusion.6, bf16[4,512,128]{2,1,0:T(8,128)(2,1)} %get-tuple-element.132, s32[]{:T(128)S(6)} %copy.12), kind=kOutput, calls=%fused_computation.clone.1 | convolution fusion | flops 1094713344 | bytes 10651652 | tf_op jit(solution)/shard_map/while/body/eval_jaxpr/dot_general | solution.py:12
  234.8 0.0 copy-done
  234.8 11.9 %convolution_add_fusion.2 = f32[64,8192]{1,0:T(8,128)S(1)} fusion(bf16[512,8192]{1,0:T(8,128)(2,1)} %exponential_convert_fusion.2, f32[64,8192]{1,0:T(8,128)S(1)} %get-tuple-element.123, pred[]{:T(512)S(6)} %compare.3, bf16[64,8192]{1,0:T(8,128)(2,1)S(1)} %copy-done), kind=kOutput, calls=%fused_computation.1.clone.1 | convolution fusion | flops 1074823168 | bytes 13631489 | tf_op jit(solution)/shard_map/while/body/eval_jaxpr/dot_general | solution.py:51
  246.6 1.1 multiply_reduce_fusion.6
  247.7 0.0 copy-start
  247.7 9.0 %exponential_convert_fusion.2 = bf16[512,8192]{1,0:T(8,128)(2,1)} fusion(bf16[8192,128]{1,0:T(8,128)(2,1)} %get-tuple-element.134, f32[8192]{0:T(1024)S(1)} %get-tuple-element.133, f32[512]{0:T(512)S(1)} %multiply_reduce_fusion.6, bf16[4,512,128]{2,1,0:T(8,128)(2,1)} %get-tuple-element.132, s32[]{:T(128)S(6)} %copy.12), kind=kOutput, calls=%fused_computation.clone.1 | convolution fusion | flops 1094713344 | bytes 10651652 | tf_op jit(solution)/shard_map/while/body/eval_jaxpr/dot_general | solution.py:12
  256.7 0.0 copy-done
  256.7 11.9 %convolution_add_fusion.2 = f32[64,8192]{1,0:T(8,128)S(1)} fusion(bf16[512,8192]{1,0:T(8,128)(2,1)} %exponential_convert_fusion.2, f32[64,8192]{1,0:T(8,128)S(1)} %get-tuple-element.123, pred[]{:T(512)S(6)} %compare.3, bf16[64,8192]{1,0:T(8,128)(2,1)S(1)} %copy-done), kind=kOutput, calls=%fused_computation.1.clone.1 | convolution fusion | flops 1074823168 | bytes 13631489 | tf_op jit(solution)/shard_map/while/body/eval_jaxpr/dot_general | solution.py:51
  268.6 1.1 multiply_reduce_fusion.6
  269.7 0.0 copy-start
  269.7 9.0 %exponential_convert_fusion.2 = bf16[512,8192]{1,0:T(8,128)(2,1)} fusion(bf16[8192,128]{1,0:T(8,128)(2,1)} %get-tuple-element.134, f32[8192]{0:T(1024)S(1)} %get-tuple-element.133, f32[512]{0:T(512)S(1)} %multiply_reduce_fusion.6, bf16[4,512,128]{2,1,0:T(8,128)(2,1)} %get-tuple-element.132, s32[]{:T(128)S(6)} %copy.12), kind=kOutput, calls=%fused_computation.clone.1 | convolution fusion | flops 1094713344 | bytes 10651652 | tf_op jit(solution)/shard_map/while/body/eval_jaxpr/dot_general | solution.py:12
  278.7 0.0 copy-done
  278.7 11.9 %convolution_add_fusion.2 = f32[64,8192]{1,0:T(8,128)S(1)} fusion(bf16[512,8192]{1,0:T(8,128)(2,1)} %exponential_convert_fusion.2, f32[64,8192]{1,0:T(8,128)S(1)} %get-tuple-element.123, pred[]{:T(512)S(6)} %compare.3, bf16[64,8192]{1,0:T(8,128)(2,1)S(1)} %copy-done), kind=kOutput, calls=%fused_computation.1.clone.1 | convolution fusion | flops 1074823168 | bytes 13631489 | tf_op jit(solution)/shard_map/while/body/eval_jaxpr/dot_general | solution.py:51
  290.6 85.9 %all-reduce.2 = bf16[64,8192]{1,0:T(8,128)(2,1)S(1)} all-reduce(f32[64,8192]{1,0:T(8,128)S(1)} %get-tuple-element.35), channel_id=1, replica_groups=mesh['grp'=8,'row'=32] {'grp','row'}, use_global_device_ids=true, to_apply=%region_6.7 | all-reduce | flops 524288 | bytes 3145728 | tf_op jit(solution)/shard_map/psum | solution.py:56
  376.5 4.4 fusion.3
  380.9 0.0 reduce-scatter.3.cloned.1.call-update
  380.9 0.0 reduce-scatter.5.cloned.1.call-start
  380.9 139.3 %reduce-scatter.3.cloned.1.call-done = f32[64,256]{1,0:T(8,128)} async-done(((f32[64,8192]{1,0:T(8,128)}), f32[64,256]{1,0:T(8,128)}) %reduce-scatter.3.cloned.1.call-update) | async-done | bytes 65552 | tf_op jit(solution)/shard_map/reduce_scatter | solution.py:62
  520.3 0.0 copy-start.3
  520.3 0.0 copy-start.1
  520.3 0.0 copy-start.4
  520.3 4.5 fusion.4
  524.8 0.0 reduce-scatter.5.cloned.1.call-update
  524.8 0.0 copy-done.3
  524.8 0.1 multiply_reduce_fusion.4
  524.9 144.8 %reduce-scatter.5.cloned.1.call-done = f32[64,256]{1,0:T(8,128)} async-done(((f32[64,8192]{1,0:T(8,128)}), f32[64,256]{1,0:T(8,128)}) %reduce-scatter.5.cloned.1.call-update) | async-done | bytes 65552 | tf_op jit(solution)/shard_map/reduce_scatter | solution.py:67
  669.7 0.0 copy-done.1
  669.7 0.9 multiply_reduce_fusion.3
  670.7 72.6 %all-reduce = (f32[64]{0:T(128)S(1)}, f32[64]{0:T(128)S(1)}) all-reduce(f32[64]{0:T(128)S(1)} %multiply_reduce_fusion.4, f32[64]{0:T(128)S(1)} %multiply_reduce_fusion.3), channel_id=1, replica_groups=mesh['grp'=8,'row'=32] {'row'}, use_global_device_ids=true, to_apply=%region_1.2 | all-reduce | flops 128 | bytes 1024 | tf_op jit(solution)/shard_map/psum | solution.py:68
  743.2 1.0 multiply_reduce_fusion.2
  744.3 0.0 copy-start.2
  744.3 67.9 %psum.31 = f32[64]{0:T(128)S(1)} all-reduce(f32[64]{0:T(128)S(1)} %get-tuple-element.71), channel_id=1, replica_groups=mesh['grp'=8,'row'=32] {'row'}, use_global_device_ids=true, to_apply=%region_12.13 | all-reduce | flops 64 | bytes 512 | tf_op jit(solution)/shard_map/psum | solution.py:72
  812.1 0.0 copy-done.4
  812.1 0.7 multiply_add_fusion
  812.9 0.0 copy-done.2
  (3 shorter events, 0.0 us)
Async XLA Ops:
  7.2 67.6 %all-gather.4.cloned.1.call-start = ((), (), s32[]{:S(2)}) async-start(), calls=%async_computation.2 | async-start | bytes 1081344 | tf_op jit(solution)/shard_map/all_gather | solution.py:26
  8.7 130.0 %all-gather.6.cloned.1.call-start = ((), (), s32[]{:S(2)}) async-start(), calls=%async_computation.3 | async-start | bytes 1081344 | tf_op jit(solution)/shard_map/all_gather | solution.py:34
  79.3 123.4 %all-gather.8.cloned.1.call-start = ((), (), s32[]{:S(2)}) async-start(), calls=%async_computation.4 | async-start | bytes 1081344 | tf_op jit(solution)/shard_map/all_gather | solution.py:39
  143.3 377.0 %reduce-scatter.3.cloned.1.call-start = ((), (), s32[]{:S(2)}) async-start(), calls=%async_computation.5 | async-start | bytes 2162688 | tf_op jit(solution)/shard_map/reduce_scatter | solution.py:62
  203.7 9.1 %copy-start = (bf16[64,8192]{1,0:T(8,128)(2,1)S(1)}, bf16[64,8192]{1,0:T(8,128)(2,1)}, u32[]{:S(2)}) copy-start(bf16[64,8192]{1,0:T(8,128)(2,1)} %get-tuple-element.135) | copy-start | bytes 3145732 | tf_op jit(solution)/shard_map/while
  225.7 9.1 %copy-start = (bf16[64,8192]{1,0:T(8,128)(2,1)S(1)}, bf16[64,8192]{1,0:T(8,128)(2,1)}, u32[]{:S(2)}) copy-start(bf16[64,8192]{1,0:T(8,128)(2,1)} %get-tuple-element.135) | copy-start | bytes 3145732 | tf_op jit(solution)/shard_map/while
  247.7 9.1 %copy-start = (bf16[64,8192]{1,0:T(8,128)(2,1)S(1)}, bf16[64,8192]{1,0:T(8,128)(2,1)}, u32[]{:S(2)}) copy-start(bf16[64,8192]{1,0:T(8,128)(2,1)} %get-tuple-element.135) | copy-start | bytes 3145732 | tf_op jit(solution)/shard_map/while
  269.7 9.1 %copy-start = (bf16[64,8192]{1,0:T(8,128)(2,1)S(1)}, bf16[64,8192]{1,0:T(8,128)(2,1)}, u32[]{:S(2)}) copy-start(bf16[64,8192]{1,0:T(8,128)(2,1)} %get-tuple-element.135) | copy-start | bytes 3145732 | tf_op jit(solution)/shard_map/while
  380.9 288.8 %reduce-scatter.5.cloned.1.call-start = ((), (), s32[]{:S(2)}) async-start(), calls=%async_computation.6 | async-start | bytes 2162688 | tf_op jit(solution)/shard_map/reduce_scatter | solution.py:67
  520.3 4.5 copy-start.3
  520.3 149.4 %copy-start.1 = (f32[64,256]{1,0:T(8,128)S(1)}, f32[64,256]{1,0:T(8,128)}, u32[]{:S(2)}) copy-start(f32[64,256]{1,0:T(8,128)} %param.15) | copy-start | bytes 196612
  520.3 291.8 %copy-start.4 = (f32[64,256]{1,0:T(8,128)S(1)}, f32[64,256]{1,0:T(8,128)}, u32[]{:S(2)}) copy-start(f32[64,256]{1,0:T(8,128)} %param.13) | copy-start | bytes 196612
  744.3 68.6 %copy-start.2 = (f32[64,256]{1,0:T(8,128)}, f32[64,256]{1,0:T(8,128)S(1)}, u32[]{:S(2)}) copy-start(f32[64,256]{1,0:T(8,128)S(1)} %get-tuple-element.72) | copy-start | bytes 196612
Sparse Core Ops, SparseCore 0:
  10.3 64.4 all-gather.3
  79.4 59.2 all-gather.5
  143.4 59.2 all-gather.7
  381.0 139.2 reduce-scatter.2
  524.9 144.7 reduce-scatter.4
where the time goes:
time: 820 us; the launch traced here: 819 us
  waiting for transfers between devices  466 us (57%)
  blocking collectives  226 us (28%)
  matrix products  101 us (12%)
  between operations  13.8 us (2%)
  other arithmetic  11.2 us (1%)
    reduce_scatter x1, waiting for transfers between devices, local(): lax.psum_scatter(inner_terms, 'row', scatter_dimension=1, tiled=True)  145 us
    reduce_scatter x1, waiting for transfers between devices, local(): lax.psum_scatter(outer_terms, 'row', scatter_dimension=1, tiled=True)  139 us
    psum x1, blocking collectives, local(): summed_all = lax.psum(partial_sums, ('grp', 'row'))  85.9 us
    psum x1, blocking collectives, local(): old_norm = lax.psum(jnp.sum(residual * residual, axis=1), 'row')  72.6 us
    psum x1, blocking collectives, local(): new_norm = lax.psum(jnp.sum(next_residual * next_residual, axis=1), 'row')  67.9 us
    all_gather x1, waiting for transfers between devices, local(): lax.all_gather(direction_half, 'row', axis=1, tiled=True)  66 us
    all_gather x1, waiting for transfers between devices, local(): lax.all_gather(inner_half, 'row', axis=1, tiled=True)  59.4 us
    all_gather x1, waiting for transfers between devices, local(): lax.all_gather(outer_rows.astype(jnp.bfloat16), 'row', axis=1, tiled=True)  56.4 us
  transfers between devices with their start and end apart: 5, of which 5 were waited for; matrix products, arithmetic and copies ran while one was open for 0% of the time, Pallas kernels for 0%

commit v1 on v0

--- a/solution.py
+++ b/solution.py
@@ -4,6 +4,7 @@
 from jax.sharding import PartitionSpec as P
 
 ridge_weight = 0.5
+assign_view = lambda page: lax.psum(lax.psum(page, "row"), "grp")
 
 
 def kernel_rows(block_points, centers, center_norms):
@@ -53,7 +54,7 @@
     partial_sums, _ = lax.scan(
         one_block, jnp.zeros((targets, centers.shape[0]), jnp.float32), point_blocks
     )
-    summed_all = lax.psum(partial_sums, ("grp", "row"))
+    summed_all = assign_view(partial_sums)
     own_normal = lax.dynamic_slice_in_dim(summed_all, lax.axis_index("row") * own_rows, own_rows, 1)
     normal_half = own_normal.astype(jnp.bfloat16)
     point_count = local_points * lax.axis_size("grp") * lax.axis_size("row")

time: 820 us -> 1130 us (1.38)
  waiting for transfers between devices: 466 us -> 760 us
  blocking collectives: 226 us -> 246 us
    psum x0 -> x1, waiting for transfers between devices: none -> 283 us  [assign_view = lambda page: lax.psum(lax.psum(page, 'row'), 'grp')]
    psum x1, blocking collectives: 85.9 us -> 106 us  [assign_view = lambda page: lax.psum(lax.psum(page, 'row'), 'grp')]
  transfers between devices with their start and end apart: 5 -> 6, of which waited for: 5 -> 6; matrix products, arithmetic and copies ran while one was open for 0% -> 0% of each run, Pallas kernels for 0% -> 0%
where the time goes in v1:
time: 1130 us
  waiting for transfers between devices  760 us (67%)
  blocking collectives  246 us (22%)
  matrix products  101 us (9%)
  between operations  14.2 us (1%)
    psum x1, waiting for transfers between devices, assign_view = lambda page: lax.psum(lax.psum(page, 'row'), 'grp')  283 us
    reduce_scatter x1, waiting for transfers between devices, local(): lax.psum_scatter(outer_terms, 'row', scatter_dimension=1, tiled=True)  150 us
    reduce_scatter x1, waiting for transfers between devices, local(): lax.psum_scatter(inner_terms, 'row', scatter_dimension=1, tiled=True)  145 us
    psum x1, blocking collectives, assign_view = lambda page: lax.psum(lax.psum(page, 'row'), 'grp')  106 us
    psum x1, blocking collectives, local(): old_norm = lax.psum(jnp.sum(residual * residual, axis=1), 'row')  72.6 us
    psum x1, blocking collectives, local(): new_norm = lax.psum(jnp.sum(next_residual * next_residual, axis=1), 'row')  67.8 us
    all_gather x1, waiting for transfers between devices, local(): lax.all_gather(direction_half, 'row', axis=1, tiled=True)  66 us
    all_gather x1, waiting for transfers between devices, local(): lax.all_gather(inner_half, 'row', axis=1, tiled=True)  59.4 us
  transfers between devices with their start and end apart: 6, of which 6 were waited for; matrix products, arithmetic and copies ran while one was open for 0% of the time, Pallas kernels for 0%

profile of v1, /device:TPU:1, one launch (start us, length us, event | category | flops | bytes accessed | tf_op | source)
XLA Modules:
  0.0 1134.5 jit_solution(246825405639956224)
XLA Ops:
  7.2 0.0 all-gather.4.cloned.1.call-start
  7.2 1.5 convert_element_type.29
  8.7 0.0 all-gather.4.cloned.1.call-update
  8.7 0.0 all-gather.6.cloned.1.call-start
  8.7 66.0 %all-gather.4.cloned.1.call-done = bf16[64,8192]{1,0:T(8,128)(2,1)} async-done(((bf16[64,256]{1,0:T(8,128)(2,1)}), bf16[64,8192]{1,0:T(8,128)(2,1)}) %all-gather.4.cloned.1.call-update) | async-done | bytes 1048592 | tf_op jit(solution)/shard_map/all_gather | solution.py:27
  74.8 4.5 fusion.10
  79.3 0.0 all-gather.6.cloned.1.call-update
  79.3 0.0 all-gather.8.cloned.1.call-start
  79.4 59.4 %all-gather.6.cloned.1.call-done = bf16[64,8192]{1,0:T(8,128)(2,1)} async-done(((bf16[64,256]{1,0:T(8,128)(2,1)}), bf16[64,8192]{1,0:T(8,128)(2,1)}) %all-gather.6.cloned.1.call-update) | async-done | bytes 1048592 | tf_op jit(solution)/shard_map/all_gather | solution.py:35
  138.7 4.5 convolution_convert_fusion.1
  143.2 0.0 all-gather.8.cloned.1.call-update
  143.3 0.0 all-reduce.4.cloned.1.call-start
  143.3 2.7 multiply_reduce_fusion.1
  146.1 56.6 %all-gather.8.cloned.1.call-done = bf16[64,8192]{1,0:T(8,128)(2,1)} async-done(((bf16[64,256]{1,0:T(8,128)(2,1)}), bf16[64,8192]{1,0:T(8,128)(2,1)}) %all-gather.8.cloned.1.call-update) | async-done | bytes 1048592 | tf_op jit(solution)/shard_map/all_gather | solution.py:40
  202.7 87.9 %while.11 = (s32[]{:T(128)}, f32[64,8192]{1,0:T(8,128)S(1)}, bf16[4,512,128]{2,1,0:T(8,128)(2,1)}, f32[8192]{0:T(1024)S(1)}, bf16[8192,128]{1,0:T(8,128)(2,1)}, ...) while((s32[]{:T(128)}, f32[64,8192]{1,0:T(8,128)S(1)}, bf16[4,512,128]{2,1,0:T(8,128)(2,1)}, ...), condition=%wide.region_5.6_spmd.clone, body=%wide.region_3.0_spmd.clone.sunk | while | flops 2169732608 | bytes 28610700 | solution.py:54
  202.7 1.0 multiply_reduce_fusion.6
  203.7 0.0 copy-start.1
  203.7 9.1 exponential_convert_fusion.2
  212.8 0.0 copy-done.1
  212.8 11.9 %convolution_add_fusion.2 = f32[64,8192]{1,0:T(8,128)S(1)} fusion(bf16[512,8192]{1,0:T(8,128)(2,1)} %exponential_convert_fusion.2, f32[64,8192]{1,0:T(8,128)S(1)} %get-tuple-element.123, pred[]{:T(512)S(6)} %compare.3, bf16[64,8192]{1,0:T(8,128)(2,1)S(1)} %copy-done.1), kind=kOutput, calls=%fused_computation.1.clone.1 | convolution fusion | flops 1074823168 | bytes 13631489 | tf_op jit(solution)/shard_map/while/body/eval_jaxpr/dot_general | solution.py:52
  224.7 1.1 multiply_reduce_fusion.6
  225.7 0.0 copy-start.1
  225.7 9.0 exponential_convert_fusion.2
  234.8 0.0 copy-done.1
  234.8 11.9 %convolution_add_fusion.2 = f32[64,8192]{1,0:T(8,128)S(1)} fusion(bf16[512,8192]{1,0:T(8,128)(2,1)} %exponential_convert_fusion.2, f32[64,8192]{1,0:T(8,128)S(1)} %get-tuple-element.123, pred[]{:T(512)S(6)} %compare.3, bf16[64,8192]{1,0:T(8,128)(2,1)S(1)} %copy-done.1), kind=kOutput, calls=%fused_computation.1.clone.1 | convolution fusion | flops 1074823168 | bytes 13631489 | tf_op jit(solution)/shard_map/while/body/eval_jaxpr/dot_general | solution.py:52
  246.6 1.1 multiply_reduce_fusion.6
  247.7 0.0 copy-start.1
  247.7 9.0 exponential_convert_fusion.2
  256.8 0.0 copy-done.1
  256.8 11.9 %convolution_add_fusion.2 = f32[64,8192]{1,0:T(8,128)S(1)} fusion(bf16[512,8192]{1,0:T(8,128)(2,1)} %exponential_convert_fusion.2, f32[64,8192]{1,0:T(8,128)S(1)} %get-tuple-element.123, pred[]{:T(512)S(6)} %compare.3, bf16[64,8192]{1,0:T(8,128)(2,1)S(1)} %copy-done.1), kind=kOutput, calls=%fused_computation.1.clone.1 | convolution fusion | flops 1074823168 | bytes 13631489 | tf_op jit(solution)/shard_map/while/body/eval_jaxpr/dot_general | solution.py:52
  268.6 1.1 multiply_reduce_fusion.6
  269.7 0.0 copy-start.1
  269.7 9.0 exponential_convert_fusion.2
  278.7 0.0 copy-done.1
  278.7 11.9 %convolution_add_fusion.2 = f32[64,8192]{1,0:T(8,128)S(1)} fusion(bf16[512,8192]{1,0:T(8,128)(2,1)} %exponential_convert_fusion.2, f32[64,8192]{1,0:T(8,128)S(1)} %get-tuple-element.123, pred[]{:T(512)S(6)} %compare.3, bf16[64,8192]{1,0:T(8,128)(2,1)S(1)} %copy-done.1), kind=kOutput, calls=%fused_computation.1.clone.1 | convolution fusion | flops 1074823168 | bytes 13631489 | tf_op jit(solution)/shard_map/while/body/eval_jaxpr/dot_general | solution.py:52
  290.6 0.0 copy-start
  290.6 1.3 copy-done
  291.9 0.0 all-reduce.4.cloned.1.call-update
  291.9 0.0 reduce-scatter.3.cloned.1.call-start
  292.0 282.9 %all-reduce.4.cloned.1.call-done = f32[64,8192]{1,0:T(8,128)} async-done(((f32[64,8192]{1,0:T(8,128)}), f32[64,8192]{1,0:T(8,128)}) %all-reduce.4.cloned.1.call-update) | async-done | bytes 2097168 | tf_op jit(solution)/shard_map/psum | solution.py:7
  574.9 105.8 %all-reduce.5 = bf16[64,8192]{1,0:T(8,128)(2,1)S(1)} all-reduce(f32[64,8192]{1,0:T(8,128)} %all-reduce.4.cloned.1.call-done), channel_id=1, replica_groups=mesh['grp'=8,'row'=32] {'grp'}, use_global_device_ids=true, to_apply=%region_7.8 | all-reduce | flops 524288 | bytes 3145728 | tf_op jit(solution)/shard_map/psum | solution.py:7
  680.7 4.4 fusion.3
  685.1 0.0 reduce-scatter.3.cloned.1.call-update
  685.1 0.0 reduce-scatter.5.cloned.1.call-start
  685.2 149.8 %reduce-scatter.3.cloned.1.call-done = f32[64,256]{1,0:T(8,128)} async-done(((f32[64,8192]{1,0:T(8,128)}), f32[64,256]{1,0:T(8,128)}) %reduce-scatter.3.cloned.1.call-update) | async-done | bytes 65552 | tf_op jit(solution)/shard_map/reduce_scatter | solution.py:63
  835.0 0.0 copy-start.4
  835.0 0.0 copy-start.2
  835.0 0.0 copy-start.5
  835.0 4.5 fusion.4
  839.5 0.0 reduce-scatter.5.cloned.1.call-update
  839.5 0.0 copy-done.4
  839.5 0.1 multiply_reduce_fusion.4
  839.6 144.8 %reduce-scatter.5.cloned.1.call-done = f32[64,256]{1,0:T(8,128)} async-done(((f32[64,8192]{1,0:T(8,128)}), f32[64,256]{1,0:T(8,128)}) %reduce-scatter.5.cloned.1.call-update) | async-done | bytes 65552 | tf_op jit(solution)/shard_map/reduce_scatter | solution.py:68
  984.4 0.0 copy-done.2
  984.4 0.9 multiply_reduce_fusion.3
  985.4 72.6 %all-reduce = (f32[64]{0:T(128)S(1)}, f32[64]{0:T(128)S(1)}) all-reduce(f32[64]{0:T(128)S(1)} %multiply_reduce_fusion.4, f32[64]{0:T(128)S(1)} %multiply_reduce_fusion.3), channel_id=1, replica_groups=mesh['grp'=8,'row'=32] {'row'}, use_global_device_ids=true, to_apply=%region_1.2 | all-reduce | flops 128 | bytes 1024 | tf_op jit(solution)/shard_map/psum | solution.py:69
  1058.0 1.0 multiply_reduce_fusion.2
  1059.0 0.0 copy-start.3
  1059.0 67.8 %psum.39 = f32[64]{0:T(128)S(1)} all-reduce(f32[64]{0:T(128)S(1)} %get-tuple-element.71), channel_id=1, replica_groups=mesh['grp'=8,'row'=32] {'row'}, use_global_device_ids=true, to_apply=%region_13.14 | all-reduce | flops 64 | bytes 512 | tf_op jit(solution)/shard_map/psum | solution.py:73
  1126.9 0.0 copy-done.5
  1126.9 0.7 multiply_add_fusion
  1127.6 0.0 copy-done.3
  (3 shorter events, 0.0 us)
Async XLA Ops:
  7.2 67.6 %all-gather.4.cloned.1.call-start = ((), (), s32[]{:S(2)}) async-start(), calls=%async_computation.2 | async-start | bytes 1081344 | tf_op jit(solution)/shard_map/all_gather | solution.py:27
  8.7 130.0 %all-gather.6.cloned.1.call-start = ((), (), s32[]{:S(2)}) async-start(), calls=%async_computation.3 | async-start | bytes 1081344 | tf_op jit(solution)/shard_map/all_gather | solution.py:35
  79.3 123.4 %all-gather.8.cloned.1.call-start = ((), (), s32[]{:S(2)}) async-start(), calls=%async_computation.4 | async-start | bytes 1081344 | tf_op jit(solution)/shard_map/all_gather | solution.py:40
  143.3 431.6 %all-reduce.4.cloned.1.call-start = ((), (), s32[]{:S(2)}) async-start(), calls=%async_computation.5 | async-start | bytes 4194304 | tf_op jit(solution)/shard_map/psum | solution.py:7
  203.7 9.1 copy-start.1
  225.7 9.1 copy-start.1
  247.7 9.1 copy-start.1
  269.7 9.1 copy-start.1
  290.6 1.3 copy-start
  291.9 543.1 %reduce-scatter.3.cloned.1.call-start = ((), (), s32[]{:S(2)}) async-start(), calls=%async_computation.6 | async-start | bytes 2162688 | tf_op jit(solution)/shard_map/reduce_scatter | solution.py:63
  685.1 299.3 %reduce-scatter.5.cloned.1.call-start = ((), (), s32[]{:S(2)}) async-start(), calls=%async_computation.7 | async-start | bytes 2162688 | tf_op jit(solution)/shard_map/reduce_scatter | solution.py:68
  835.0 4.5 copy-start.4
  835.0 149.4 %copy-start.2 = (f32[64,256]{1,0:T(8,128)S(1)}, f32[64,256]{1,0:T(8,128)}, u32[]{:S(2)}) copy-start(f32[64,256]{1,0:T(8,128)} %param.15) | copy-start | bytes 196612
  835.0 291.9 %copy-start.5 = (f32[64,256]{1,0:T(8,128)S(1)}, f32[64,256]{1,0:T(8,128)}, u32[]{:S(2)}) copy-start(f32[64,256]{1,0:T(8,128)} %param.13) | copy-start | bytes 196612
  1059.0 68.6 %copy-start.3 = (f32[64,256]{1,0:T(8,128)}, f32[64,256]{1,0:T(8,128)S(1)}, u32[]{:S(2)}) copy-start(f32[64,256]{1,0:T(8,128)S(1)} %get-tuple-element.72) | copy-start | bytes 196612
Sparse Core Ops, SparseCore 0:
  10.3 64.4 all-gather.3
  79.4 59.2 all-gather.5
  143.4 59.2 all-gather.7
  292.1 282.7 all-reduce.3
  685.3 149.6 reduce-scatter.2
  839.6 144.7 reduce-scatter.4
